TPU v7x, 256 devices: a whole 4x4x8 slice. The times are simulated.
256 devices in a mesh: ctx: 32 (over x, z), head: 8 (over y, core).
Axes of the slice: x: 4, y: 4, z: 8, core: 2. Of those that a mesh axis runs over, the one named last changes fastest.
Arguments:
- keys: bfloat16 [65536, 5120], P('ctx', 'head'), may hold values from -6 to 6
- values: bfloat16 [65536, 5120], P('ctx', 'head'), may hold values from -6 to 6
- queries: bfloat16 [65536, 5120], P('ctx', 'head'), may hold values from -6 to 6
- rates: float32 [65536, 16], P('ctx', 'head'), may hold values from 9.765625e-05 to 0.0009765625
- w_gate: bfloat16 [320, 16, 320], P('ctx', 'head'), may hold values from -0.3125 to 0.3125
- w_up: bfloat16 [320, 16, 320], P('ctx', 'head'), may hold values from -0.3125 to 0.3125
- w_down: bfloat16 [320, 16, 320], P('ctx', 'head'), may hold values from -0.3125 to 0.3125
- gain: float32 [5120], P('head'), may hold values from 0.5 to 1.5
Outputs:
- output: bfloat16 [65536, 5120], P('ctx', 'head')
- new_gate: bfloat16 [320, 16, 320], P('ctx', 'head')
- new_up: bfloat16 [320, 16, 320], P('ctx', 'head')
- new_down: bfloat16 [320, 16, 320], P('ctx', 'head')
All inputs are finite; a program needn't handle non-finite values.
Results may differ from a plain program's by a relative error of at most 0.0092.
Values may be sent and summed in bfloat16 or wider, within the bound.
No kernel may reach another device: no remote copies, remote signals or barrier semaphores. Data moves between devices by JAX's collectives and lax.ppermute only.
A program may use at most 128 MiB of HBM per device.

v0:
```python
import jax
import jax.numpy as jnp
from jax import lax
from jax.sharding import PartitionSpec as P

HEADS = 16
DH = 320
EPS = 1e-06


def joined_along(pieces, dim):
    dims = list(pieces.shape[1:])
    dims[dim] *= pieces.shape[0]
    return jnp.moveaxis(pieces, 0, dim).reshape(dims)


def from_everyone(array, axis):
    peers = lax.axis_size(axis)
    return lax.all_to_all(
        jnp.broadcast_to(array[None], (peers, *array.shape)), axis, 0, 0, tiled=True
    )


def gather_directly(array, axis, dim):
    return joined_along(from_everyone(array, axis), dim)


def sent_together(arrays, axis, dim, along):
    ends, at = ([], 0)
    for a in arrays[:-1]:
        at += a.shape[along]
        ends.append(at)
    both = jnp.concatenate(arrays, axis=along)
    return tuple(jnp.split(gather_directly(both, axis, dim), ends, axis=along))


def taken_together(array, axis):
    everything = from_everyone(array, axis)
    return jnp.sum(everything, axis=0)


def per_device(keys, values, queries, rates, w_gate, w_up, w_down, gain):
    rows = keys.shape[0]
    heads = w_gate.shape[1]
    width = w_gate.shape[2]
    local_units = w_gate.shape[0]
    keyh = keys.reshape(rows, heads, width)
    valueh = values.reshape(rows, heads, width)
    queryh = queries.reshape(rows, heads, width)
    full_gate, full_up, full_down = sent_together((w_gate, w_up, w_down), "ctx", 0, 1)
    gpre = jnp.einsum("thd,fhd->thf", keyh, full_gate, preferred_element_type=jnp.float32)
    upre = jnp.einsum("thd,fhd->thf", keyh, full_up, preferred_element_type=jnp.float32)
    sig = jax.nn.sigmoid(gpre)
    act = gpre * sig
    slope = sig * (1.0 + gpre * (1.0 - sig))
    hidden = (act * upre).astype(jnp.bfloat16)
    scaled = (valueh.astype(jnp.float32) * rates[:, :, None]).astype(jnp.bfloat16)
    back = jnp.einsum("thd,fhd->thf", scaled, full_down, preferred_element_type=jnp.float32)
    dgate = (back * upre * slope).astype(jnp.bfloat16)
    dup = (back * act).astype(jnp.bfloat16)
    grad_gate = jnp.einsum("thf,thd->fhd", dgate, keyh, preferred_element_type=jnp.float32)
    grad_up = jnp.einsum("thf,thd->fhd", dup, keyh, preferred_element_type=jnp.float32)
    grad_down = jnp.einsum("thf,thd->fhd", hidden, scaled, preferred_element_type=jnp.float32)
    total = lax.psum(jnp.stack([grad_gate, grad_up, grad_down], axis=1), "ctx")
    olds = jnp.stack([full_gate, full_up, full_down], axis=1).astype(jnp.float32)
    updated = olds + total
    old_sq = jnp.sum(olds * olds, axis=0)
    new_sq = jnp.sum(updated * updated, axis=0)
    fresh = (updated * (jnp.sqrt(old_sq) * lax.rsqrt(new_sq + EPS))[None]).astype(jnp.bfloat16)
    offset = lax.axis_index("ctx") * local_units
    mine = lax.dynamic_slice_in_dim(fresh, offset, local_units, 0)
    new_gate = fresh[:, 0]
    new_up = fresh[:, 1]
    new_down = fresh[:, 2]
    qgate = jnp.einsum("thd,fhd->thf", queryh, new_gate, preferred_element_type=jnp.float32)
    qup = jnp.einsum("thd,fhd->thf", queryh, new_up, preferred_element_type=jnp.float32)
    mixed = (jax.nn.silu(qgate) * qup).astype(jnp.bfloat16)
    outh = jnp.einsum("thf,fhd->thd", mixed, new_down, preferred_element_type=jnp.float32)
    squares = taken_together(jnp.sum(outh * outh, axis=(1, 2)), "head")
    scale = lax.rsqrt(squares / (HEADS * DH) + EPS)
    result = outh * scale[:, None, None] * gain.reshape(heads, width)[None]
    output = result.reshape(rows, heads * width).astype(jnp.bfloat16)
    return (output, mine[:, 0], mine[:, 1], mine[:, 2])


def solution(mesh):
    in_specs = (
        P("ctx", "head"),
        P("ctx", "head"),
        P("ctx", "head"),
        P("ctx", "head"),
        P("ctx", "head", None),
        P("ctx", "head", None),
        P("ctx", "head", None),
        P("head"),
    )
    out_specs = (
        P("ctx", "head"),
        P("ctx", "head", None),
        P("ctx", "head", None),
        P("ctx", "head", None),
    )
    return jax.shard_map(
        per_device, mesh=mesh, in_specs=in_specs, out_specs=out_specs, check_vma=False
    )
```

profile of v0, /device:TPU:1, one launch (start us, length us, event | category | flops | bytes accessed | tf_op | source)
XLA Modules:
  0.0 292.5 jit_solution(10349840413681517928)
XLA Ops:
  7.2 0.8 pad_maximum_fusion.2
  8.0 1.4 broadcast_in_dim.4
  9.4 12.0 %all-to-all-start = ((bf16[32,10,6,320]{3,2,1,0:T(8,128)(2,1)}), bf16[32,10,6,320]{3,2,1,0:T(8,128)(2,1)}, u32[]{:S(2)}, u32[]{:S(2)}) async-start(bf16[32,10,6,320]{3,2,1,0:T(8,128)(2,1)} %broadcast_in_dim.4), calls=%async_computation | async-start | bytes 3932160 | tf_op jit(solution)/shard_map/all_to_all | solution.py:19
  21.4 0.0 all-reduce.2.cloned.1.call-start
  21.4 3.0 %copy.53 = bf16[2048,640]{0,1:T(8,128)(2,1)S(1)} copy(bf16[2048,640]{1,0:T(8,128)(2,1)} %param.8) | data formatting | bytes 5242880 | tf_op args[0]
  24.4 4.4 %copy.52 = bf16[2048,640]{0,1:T(8,128)(2,1)} copy(bf16[2048,640]{1,0:T(8,128)(2,1)} %param.9) | data formatting | bytes 5242880 | tf_op args[1]
  28.8 38.8 %all-to-all-done = bf16[32,10,6,320]{3,2,1,0:T(8,128)(2,1)} async-done(((bf16[32,10,6,320]{3,2,1,0:T(8,128)(2,1)}), bf16[32,10,6,320]{3,2,1,0:T(8,128)(2,1)}, u32[]{:S(2)}, u32[]{:S(2)}) %all-to-all-start) | async-done | bytes 1228832 | tf_op jit(solution)/shard_map/all_to_all | solution.py:19
  67.6 4.1 %fusion.46 = (bf16[320,2,320]{2,1,0:T(2,128)(2,1)S(1)}, bf16[320,2,320]{2,1,0:T(2,128)(2,1)S(1)}, bf16[320,2,320]{2,1,0:T(2,128)(2,1)S(1)}) fusion(bf16[320,6,320]{2,1,0:T(8,128)(2,1)} %bitcast), kind=kLoop, calls=%fused_computation.63 | loop fusion | bytes 2457600 | tf_op jit(solution)/shard_map/split | solution.py:34
  71.8 0.0 copy-start.4
  71.8 0.0 copy-start.3
  71.8 1.5 fusion.40
  73.3 0.0 copy-done.4
  73.3 0.0 copy-start.1
  73.3 0.0 copy-start.10
  73.4 3.8 %fusion.38 = f32[2,320,2048]{2,1,0:T(8,128)} fusion(bf16[2048,2,320]{0,2,1:T(8,128)(2,1)S(1)} %bitcast.134, bf16[320,2,320]{2,1,0:T(2,128)(2,1)S(1)} %get-tuple-element.23), kind=kOutput, calls=%fused_computation.47 | convolution fusion | flops 838860800 | bytes 8273920 | tf_op jit(solution)/shard_map/thd,fhd->thf/dot_general | solution.py:52
  77.2 1.5 fusion.22
  78.7 2.3 copy-done.2
  81.1 1.7 fusion.33
  82.7 7.2 %fusion.25 = f32[320,1,2,320]{3,0,2,1:T(8,128)} fusion(bf16[2048,2,320]{0,2,1:T(8,128)(2,1)S(1)} %bitcast.136, f32[2,320,2048]{2,1,0:T(8,128)S(1)} %fusion.40, f32[2,320,2048]{2,1,0:T(8,128)} %fusion.38, f32[2,320,2048]{2,1,0:T(8,128)} %copy-done.2), kind=kOutput, calls=%fused_computation.38 | convolution fusion | flops 851968000 | bytes 19169280 | tf_op jit(solution)/shard_map/thf,thd->fhd/dot_general | solution.py:61
  89.9 4.3 %fusion.28 = f32[320,1,2,320]{3,0,2,1:T(8,128)S(1)} fusion(f32[2,320,2048]{2,1,0:T(8,128)} %fusion.38, bf16[2048,2,320]{0,2,1:T(8,128)(2,1)S(1)} %bitcast.140, f32[2048,2]{0,1:T(2,128)S(1)} %copy-done.10, f32[2,320,2048]{2,1,0:T(8,128)S(1)} %fusion.40), kind=kOutput, calls=%fused_computation.39 | convolution fusion | flops 850657280 | bytes 13942784 | tf_op jit(solution)/shard_map/thf,thd->fhd/dot_general | solution.py:63
  94.2 1.8 pad_maximum_fusion
  96.0 0.0 all-reduce.2.cloned.1.call-update
  96.0 0.0 copy-start.11
  96.1 3.2 %copy.55 = bf16[2048,640]{0,1:T(8,128)(2,1)S(1)} copy(bf16[2048,640]{1,0:T(8,128)(2,1)} %param.10) | data formatting | bytes 5242880 | tf_op args[2]
  99.3 0.1 mul.103
  99.3 0.8 copy.77
  100.2 2.3 copy_bitcast_fusion
  102.5 146.1 %all-reduce.2.cloned.1.call-done = f32[320,3,2,320]{3,0,2,1:T(8,128)} async-done(((f32[320,3,2,320]{3,0,2,1:T(8,128)}), f32[320,3,2,320]{3,0,2,1:T(8,128)}) %all-reduce.2.cloned.1.call-update) | async-done | bytes 2457616 | tf_op jit(solution)/shard_map/psum | solution.py:64
  248.6 3.1 %fusion.14 = (f32[3,2,320]{2,1,0:T(2,128)S(1)}, f32[3,2,320]{2,1,0:T(2,128)S(1)}) fusion(bf16[320,1,2,320]{3,0,2,1:T(8,128)(2,1)} %get-tuple-element.30, bf16[320,1,2,320]{3,0,2,1:T(8,128)(2,1)} %get-tuple-element.31, bf16[320,1,2,320]{3,0,2,1:T(8,128)(2,1)} %bitcast.142, f32[320,3,2,320]{3,0,2,1:T(8,128)} %all-reduce.2.cloned.1.call-done), kind=kLoop, calls=%fused_computation.28 | loop fusion | flops 4911360 | bytes 3701760 | tf_op jit(solution)/shard_map/reduce_sum | solution.py:67
  251.8 0.0 copy-done.5
  251.8 0.0 copy-done
  251.8 0.1 copy-done.6
  251.9 0.1 copy-done.7
  252.0 0.5 multiply_convert_fusion.1
  252.5 0.0 copy-start.8
  252.5 1.1 copy-done.8
  253.6 3.9 %fusion.36 = f32[2,320,2048]{2,1,0:T(8,128)} fusion(bf16[2048,2,320]{0,2,1:T(8,128)(2,1)S(1)} %bitcast.137, bf16[320,3,2,320]{3,0,2,1:T(8,128)(2,1)S(1)} %multiply_convert_fusion.1), kind=kOutput, calls=%fused_computation.43 | convolution fusion | flops 838860800 | bytes 8355840 | tf_op jit(solution)/shard_map/thd,fhd->thf/dot_general | solution.py:75
  257.5 8.4 %multiply_reduce_fusion = (f32[2048]{0:T(1024)S(1)}, f32[2,320,2048]{2,1,0:T(8,128)}) fusion(f32[2,320,2048]{2,1,0:T(8,128)} %fusion.36, bf16[2048,2,320]{0,2,1:T(8,128)(2,1)S(1)} %bitcast.138, bf16[320,3,2,320]{3,0,2,1:T(8,128)(2,1)} %copy-done.8), kind=kOutput, calls=%fused_computation.25 | convolution fusion | flops 1688205312 | bytes 14098432 | tf_op jit(solution)/shard_map/thf,fhd->thd/dot_general | solution.py:78
  265.9 0.6 broadcast_in_dim.5
  266.6 8.6 %all-to-all-start.1 = ((f32[8,1,2048]{2,1,0:T(1,128)}), f32[8,1,2048]{2,1,0:T(1,128)S(1)}, u32[]{:S(2)}, u32[]{:S(2)}) async-start(f32[8,1,2048]{2,1,0:T(1,128)} %broadcast_in_dim.5), calls=%async_computation.1 | async-start | bytes 131072 | tf_op jit(solution)/shard_map/all_to_all | solution.py:19
  275.2 0.8 dynamic-slice_bitcast_fusion
  276.0 0.6 copy.59
  276.6 0.6 copy.60
  277.3 0.6 copy.61
  277.9 2.2 all-to-all-done.1
  280.0 0.1 reduce_sum.39
  280.1 3.0 %multiply_convert_fusion = bf16[2,320,2048]{2,1,0:T(8,128)(2,1)S(1)} fusion(f32[2,320,2048]{2,1,0:T(8,128)} %get-tuple-element.29, f32[2,320]{1,0:T(2,128)S(1)} %mul.103, f32[2048]{0:T(1024)S(1)} %add_rsqrt_fusion), kind=kLoop, calls=%fused_computation.24 | loop fusion | flops 3932160 | bytes 7875072 | tf_op jit(solution)/shard_map/convert_element_type | solution.py:82
  283.1 2.6 copy.58
  (13 shorter events, 0.0 us)
Async XLA Ops:
  9.4 58.2 %all-to-all-start = ((bf16[32,10,6,320]{3,2,1,0:T(8,128)(2,1)}), bf16[32,10,6,320]{3,2,1,0:T(8,128)(2,1)}, u32[]{:S(2)}, u32[]{:S(2)}) async-start(bf16[32,10,6,320]{3,2,1,0:T(8,128)(2,1)} %broadcast_in_dim.4), calls=%async_computation | async-start | bytes 3932160 | tf_op jit(solution)/shard_map/all_to_all | solution.py:19
  21.4 227.2 %all-reduce.2.cloned.1.call-start = ((), (), s32[]{:S(2)}) async-start(), calls=%async_computation.2 | async-start | bytes 5898240 | tf_op jit(solution)/shard_map/psum | solution.py:64
  71.8 1.6 copy-start.4
  71.8 5.4 %copy-start.3 = (bf16[320,2,320]{2,1,0:T(2,128)(2,1)}, bf16[320,2,320]{2,1,0:T(2,128)(2,1)S(1)}, u32[]{:S(2)}) copy-start(bf16[320,2,320]{2,1,0:T(2,128)(2,1)S(1)} %get-tuple-element.22) | copy-start | bytes 1228804
  73.3 3.8 %copy-start.1 = (bf16[2048,640]{0,1:T(8,128)(2,1)S(1)}, bf16[2048,640]{0,1:T(8,128)(2,1)}, u32[]{:S(2)}) copy-start(bf16[2048,640]{0,1:T(8,128)(2,1)} %copy.52) | copy-start | bytes 7864324
  73.3 3.8 %copy-start.10 = (f32[2048,2]{0,1:T(2,128)S(1)}, f32[2048,2]{0,1:T(2,128)}, u32[]{:S(2)}) copy-start(f32[2048,2]{0,1:T(2,128)} %param.11) | copy-start | bytes 49156
  78.7 2.3 copy-start.2
  89.9 4.3 %copy-start.9 = (f32[320,1,2,320]{3,0,2,1:T(8,128)S(1)}, f32[320,1,2,320]{3,0,2,1:T(8,128)}, u32[]{:S(2)}) copy-start(f32[320,1,2,320]{3,0,2,1:T(8,128)} %fusion.25) | copy-start | bytes 2457604
  96.0 3.2 %copy-start.11 = (f32[640]{0:T(1024)S(1)}, f32[640]{0:T(1024)}, u32[]{:S(2)}) copy-start(f32[640]{0:T(1024)} %param.15) | copy-start | bytes 7684
  100.2 151.6 %copy-start.5 = (bf16[320,2,320]{2,0,1:T(8,128)(2,1)S(1)}, bf16[320,2,320]{2,0,1:T(8,128)(2,1)}, u32[]{:S(2)}) copy-start(bf16[320,2,320]{2,0,1:T(8,128)(2,1)} %copy.77) | copy-start | bytes 1228804
  248.6 3.2 %copy-start = (f32[320,3,2,320]{3,0,2,1:T(8,128)S(1)}, f32[320,3,2,320]{3,0,2,1:T(8,128)}, u32[]{:S(2)}) copy-start(f32[320,3,2,320]{3,0,2,1:T(8,128)} %all-reduce.2.cloned.1.call-done) | copy-start | bytes 7372804
  248.6 3.2 %copy-start.6 = (bf16[320,1,2,320]{3,0,2,1:T(8,128)(2,1)S(1)}, bf16[320,1,2,320]{3,0,2,1:T(8,128)(2,1)}, u32[]{:S(2)}) copy-start(bf16[320,1,2,320]{3,0,2,1:T(8,128)(2,1)} %get-tuple-element.30) | copy-start | bytes 1228804
  248.6 3.4 %copy-start.7 = (bf16[320,1,2,320]{3,0,2,1:T(8,128)(2,1)S(1)}, bf16[320,1,2,320]{3,0,2,1:T(8,128)(2,1)}, u32[]{:S(2)}) copy-start(bf16[320,1,2,320]{3,0,2,1:T(8,128)(2,1)} %get-tuple-element.31) | copy-start | bytes 1228804
  252.5 1.1 copy-start.8
  266.6 13.5 %all-to-all-start.1 = ((f32[8,1,2048]{2,1,0:T(1,128)}), f32[8,1,2048]{2,1,0:T(1,128)S(1)}, u32[]{:S(2)}, u32[]{:S(2)}) async-start(f32[8,1,2048]{2,1,0:T(1,128)} %broadcast_in_dim.5), calls=%async_computation.1 | async-start | bytes 131072 | tf_op jit(solution)/shard_map/all_to_all | solution.py:19
Sparse Core Ops, SparseCore 0:
  96.2 152.3 all-reduce.1
where the time goes:
time: 293 us
  waiting for transfers between devices  187 us (64%)
  matrix products  32.3 us (11%)
  local copies, waits for them, and re-layouts  28.9 us (10%)
  starting transfers between devices  20.6 us (7%)
  between operations  14.2 us (5%)
  other arithmetic  9.31 us (3%)
    psum x1, waiting for transfers between devices, per_device(): total = lax.psum(jnp.stack([grad_gate, grad_up, grad_down], axis=1), 'ctx')  146 us
    all_to_all x2, waiting for transfers between devices, from_everyone(): lax.all_to_all(jnp.broadcast_to(array[None], (peers, *array.shape)), axis...  41 us
    all_to_all x2, starting transfers between devices, from_everyone(): lax.all_to_all(jnp.broadcast_to(array[None], (peers, *array.shape)), axis...  20.6 us
    unnamed x32, local copies, waits for them, and re-layouts  19.5 us
    dot_general x1, matrix products, per_device(): jnp.einsum('thf,fhd->thd', mixed, new_down, preferred_element_type=jnp.fl...  8.44 us
    dot_general x1, matrix products, per_device(): jnp.einsum('thf,thd->fhd', dgate, keyh, preferred_element_type=jnp.float32)  7.15 us
  transfers between devices with their start and end apart: 3, of which 3 were waited for; matrix products, arithmetic and copies ran while one was open for 6% of the time, Pallas kernels for 0%

commit v1 on v0

--- a/solution.py
+++ b/solution.py
@@ -61,7 +61,9 @@
     grad_gate = jnp.einsum("thf,thd->fhd", dgate, keyh, preferred_element_type=jnp.float32)
     grad_up = jnp.einsum("thf,thd->fhd", dup, keyh, preferred_element_type=jnp.float32)
     grad_down = jnp.einsum("thf,thd->fhd", hidden, scaled, preferred_element_type=jnp.float32)
-    total = lax.psum(jnp.stack([grad_gate, grad_up, grad_down], axis=1), "ctx")
+    total = jnp.sum(
+        lax.all_gather(jnp.stack([grad_gate, grad_up, grad_down], axis=1), "ctx"), axis=0
+    )
     olds = jnp.stack([full_gate, full_up, full_down], axis=1).astype(jnp.float32)
     updated = olds + total
     old_sq = jnp.sum(olds * olds, axis=0)

time: 293 us -> 757 us (2.58)
  waiting for transfers between devices: 187 us -> 626 us
  other arithmetic: 9.31 us -> 37.4 us
    all_gather x0 -> x1, waiting for transfers between devices: none -> 585 us  [per_device(): lax.all_gather(jnp.stack([grad_gate, grad_up, grad_down], axis=1), 'ctx')]
    psum x1 -> x0, waiting for transfers between devices: 146 us -> none  [per_device(): total = lax.psum(jnp.stack([grad_gate, grad_up, grad_down], axis=1), 'ctx')]
    reduce_sum x0 -> x1, other arithmetic: none -> 29.2 us  [per_device(): jnp.sum(lax.all_gather(jnp.stack([grad_gate, grad_up, grad_down], axis=1)...]
    unnamed x32 -> x38, local copies, waits for them, and re-layouts: 19.5 us -> 21.3 us
  transfers between devices with their start and end apart: 3 -> 3, of which waited for: 3 -> 3; matrix products, arithmetic and copies ran while one was open for 6% -> 2% of each run, Pallas kernels for 0% -> 0%
where the time goes in v1:
time: 757 us; the launch traced here: 756 us
  waiting for transfers between devices  626 us (83%)
  other arithmetic  37.4 us (5%)
  matrix products  32.3 us (4%)
  local copies, waits for them, and re-layouts  29.5 us (4%)
  starting transfers between devices  17.3 us (2%)
  between operations  14.3 us (2%)
    all_gather x1, waiting for transfers between devices, per_device(): lax.all_gather(jnp.stack([grad_gate, grad_up, grad_down], axis=1), 'ctx')  585 us
    all_to_all x2, waiting for transfers between devices, from_everyone(): lax.all_to_all(jnp.broadcast_to(array[None], (peers, *array.shape)), axis...  41 us
    reduce_sum x1, other arithmetic, per_device(): jnp.sum(lax.all_gather(jnp.stack([grad_gate, grad_up, grad_down], axis=1)...  29.2 us
    unnamed x38, local copies, waits for them, and re-layouts  21.3 us
    all_to_all x2, starting transfers between devices, from_everyone(): lax.all_to_all(jnp.broadcast_to(array[None], (peers, *array.shape)), axis...  17.3 us
  transfers between devices with their start and end apart: 3, of which 3 were waited for; matrix products, arithmetic and copies ran while one was open for 2% of the time, Pallas kernels for 0%

profile of v1, /device:TPU:1, one launch (start us, length us, event | category | flops | bytes accessed | tf_op | source)
XLA Modules:
  0.0 756.5 jit_solution(14609785470190497737)
XLA Ops:
  7.2 0.8 pad_maximum_fusion.2
  8.0 1.4 broadcast_in_dim.4
  9.4 12.0 %all-to-all-start = ((bf16[32,10,6,320]{3,2,1,0:T(8,128)(2,1)}), bf16[32,10,6,320]{3,2,1,0:T(8,128)(2,1)}, u32[]{:S(2)}, u32[]{:S(2)}) async-start(bf16[32,10,6,320]{3,2,1,0:T(8,128)(2,1)} %broadcast_in_dim.4), calls=%async_computation | async-start | bytes 3932160 | tf_op jit(solution)/shard_map/all_to_all | solution.py:19
  21.4 0.0 all-gather.3.cloned.1.call-start
  21.4 3.0 copy.53
  24.4 4.4 copy.52
  28.8 38.8 %all-to-all-done = bf16[32,10,6,320]{3,2,1,0:T(8,128)(2,1)} async-done(((bf16[32,10,6,320]{3,2,1,0:T(8,128)(2,1)}), bf16[32,10,6,320]{3,2,1,0:T(8,128)(2,1)}, u32[]{:S(2)}, u32[]{:S(2)}) %all-to-all-start) | async-done | bytes 1228832 | tf_op jit(solution)/shard_map/all_to_all | solution.py:19
  67.6 4.2 fusion.46
  71.8 0.0 copy-start.6
  71.8 0.0 copy-start.4
  71.8 1.5 fusion.40
  73.3 0.0 copy-start.2
  73.3 0.0 copy-start.13
  73.4 3.8 fusion.38
  77.2 0.0 copy-done.13
  77.2 1.5 fusion.22
  78.8 0.0 copy-start.3
  78.8 2.3 copy-done.3
  81.1 1.7 fusion.33
  82.8 7.1 fusion.25
  89.9 4.3 fusion.28
  94.2 1.9 pad_maximum_fusion
  96.2 0.0 all-gather.3.cloned.1.call-update
  96.2 0.0 copy-start.14
  96.2 4.5 copy.55
  100.7 0.1 mul.103
  100.8 0.9 copy.77
  101.7 1.1 copy_bitcast_fusion
  102.7 584.7 %all-gather.3.cloned.1.call-done = f32[10240,3,2,320]{3,0,2,1:T(8,128)} async-done(((f32[320,3,2,320]{3,0,2,1:T(8,128)}), f32[10240,3,2,320]{3,0,2,1:T(8,128)}) %all-gather.3.cloned.1.call-update) | async-done | bytes 78643216 | tf_op jit(solution)/shard_map/all_gather | solution.py:65
  687.4 29.2 %reduce_sum.45 = f32[320,3,2,320]{3,0,2,1:T(8,128)S(1)} reduce(f32[32,320,3,2,320]{4,1,0,3,2:T(8,128)} %bitcast.15, f32[]{:T(128)} %constant.10.clone.1), dimensions={0}, to_apply=%region_0.0 | reduce | flops 19046400 | bytes 81100800 | tf_op jit(solution)/shard_map/reduce_sum | solution.py:64
  716.6 2.0 fusion.14
  718.6 0.0 copy-start
  718.6 0.5 multiply_convert_fusion.1
  719.1 1.1 copy-done.11
  720.2 0.7 copy-done
  720.9 3.9 fusion.36
  724.7 0.0 copy-done.1
  724.7 8.4 %multiply_reduce_fusion = (f32[2048]{0:T(1024)S(1)}, f32[2,320,2048]{2,1,0:T(8,128)}) fusion(f32[2,320,2048]{2,1,0:T(8,128)} %fusion.36, bf16[2048,2,320]{0,2,1:T(8,128)(2,1)S(1)} %bitcast.139, bf16[320,3,2,320]{3,0,2,1:T(8,128)(2,1)} %copy-done.11), kind=kOutput, calls=%fused_computation.25 | convolution fusion | flops 1688205312 | bytes 14098432 | tf_op jit(solution)/shard_map/thf,fhd->thd/dot_general | solution.py:80
  733.2 0.7 broadcast_in_dim.5
  733.8 5.3 all-to-all-start.1
  739.2 0.8 dynamic-slice_bitcast_fusion
  740.0 0.6 copy.59
  740.6 0.6 copy.60
  741.2 0.6 copy.61
  741.8 2.2 all-to-all-done.1
  744.0 0.1 reduce_sum.49
  744.1 3.0 multiply_convert_fusion
  747.1 2.6 copy.58
  (20 shorter events, 0.1 us)
Async XLA Ops:
  9.4 58.2 %all-to-all-start = ((bf16[32,10,6,320]{3,2,1,0:T(8,128)(2,1)}), bf16[32,10,6,320]{3,2,1,0:T(8,128)(2,1)}, u32[]{:S(2)}, u32[]{:S(2)}) async-start(bf16[32,10,6,320]{3,2,1,0:T(8,128)(2,1)} %broadcast_in_dim.4), calls=%async_computation | async-start | bytes 3932160 | tf_op jit(solution)/shard_map/all_to_all | solution.py:19
  21.4 666.0 %all-gather.3.cloned.1.call-start = ((), (), s32[]{:S(2)}) async-start(), calls=%async_computation.2 | async-start | bytes 97320960 | tf_op jit(solution)/shard_map/all_gather | solution.py:65
  71.8 1.5 copy-start.6
  71.8 5.4 copy-start.4
  73.3 3.9 copy-start.2
  73.3 3.9 copy-start.13
  78.8 2.3 copy-start.3
  89.9 4.3 copy-start.12
  96.2 4.5 copy-start.14
  96.2 5.5 copy-start.5
  96.2 5.4 copy-start.7
  687.4 29.2 %copy-start.8 = (bf16[320,2,320]{2,0,1:T(8,128)(2,1)S(1)}, bf16[320,2,320]{2,0,1:T(8,128)(2,1)}, u32[]{:S(2)}) copy-start(bf16[320,2,320]{2,0,1:T(8,128)(2,1)} %copy.77) | copy-start | bytes 1228804
  716.5 2.0 copy-start.9
  716.5 2.0 copy-start.10
  718.6 2.3 copy-start
  719.1 1.1 copy-start.11
  720.9 3.9 copy-start.1
  733.8 10.2 %all-to-all-start.1 = ((f32[8,1,2048]{2,1,0:T(1,128)}), f32[8,1,2048]{2,1,0:T(1,128)S(1)}, u32[]{:S(2)}, u32[]{:S(2)}) async-start(f32[8,1,2048]{2,1,0:T(1,128)} %broadcast_in_dim.5), calls=%async_computation.1 | async-start | bytes 131072 | tf_op jit(solution)/shard_map/all_to_all | solution.py:19
Sparse Core Ops, SparseCore 0:
  96.3 591.0 all-gather.2
